TPU v7x, 32 devices: a whole 2x2x4 slice. The times are simulated.
32 devices in a mesh: grp: 4 (over y, core), dev: 8 (over z, x).
Axes of the slice: x: 2, y: 2, z: 4, core: 2. Of those that a mesh axis runs over, the one named last changes fastest.
Arguments:
- u_blocks: float32 [768, 32, 1024], P(('grp', 'dev')), may hold values from -20 to 20
- v_blocks: float32 [768, 32, 1024], P(('grp', 'dev')), may hold values from -0.1875 to 0.1875
- sketch: float32 [64, 32, 1024], P(('grp', 'dev')), may hold values from -6 to 6
- near_diag: float32 [64, 1024], P(('grp', 'dev')), may hold values from 0.3 to 72
- block_row: int32 [768], P(('grp', 'dev')), may hold values from 0 to 15, as said below
- col_count: int32 [64], P(('grp', 'dev')), may hold values from 8 to 12, as said below
Outputs:
- leaf_basis: float32 [64, 32, 1024], P(('grp', 'dev'))
- transfer_leaf: float32 [64, 32, 32], P(('grp', 'dev'))
- transfer_group: float32 [4, 32, 32], P('grp')
Inputs may be any that keep to these rules, and one draw needn't show every extreme that they name: A device's slots hold its blocks in the order of its column clusters, col_count[c] of them for cluster c; the remaining slots are empty. The row cluster block_row[s] belongs to device block_row[s] // 2 of the same subtree. Among the live slots of one device at most 3 have row clusters of any one device, and in every subtree some device is named by exactly 3 live slots of every device of that subtree.
All inputs are finite; a program needn't handle non-finite values.
Results may differ from a plain program's by a relative error of at most 0.0003.
Values sent between devices are 32-bit elements; how exact they have to be, the bound alone decides.
A program may use at most 128 MiB of HBM per device.

v0:
```python
import functools
import math

import jax
import jax.numpy as jnp
from jax import lax
from jax.experimental import pallas as pl
from jax.experimental.pallas import tpu as pltpu
from jax.sharding import PartitionSpec as P

F32 = jnp.float32
BF16 = jnp.bfloat16
MESH = pl.DeviceIdType.MESH
HIGHEST = lax.Precision.HIGHEST
NN = (((1,), (0,)), ((), ()))
NT = (((1,), (1,)), ((), ()))
WIDTH = 128
PAIR = 2
V_PARTS = 3


def dot(a, b, dims, precision=None):
    return lax.dot_general(a, b, dims, precision=precision, preferred_element_type=F32)


def split(x):
    high = x.astype(BF16)
    return high, (x - high.astype(F32)).astype(BF16)


def dot3(a, b, dims):
    (ah, al), (bh, bl) = a, b
    return dot(ah, bh, dims) + dot(ah, bl, dims) + dot(al, bh, dims)


def pack(square):
    rank = square.shape[0]
    return jnp.concatenate([square[i : i + 8] for i in range(0, rank, 8)], axis=1)


def unpack(packed, rank):
    return jnp.concatenate([packed[:, i * rank : (i + 1) * rank] for i in range(rank // 8)], axis=0)


def diagonal_block(square, c, rank):
    at = slice(c * rank, (c + 1) * rank)
    return square[at, at]


def factor(grams):
    rank = grams[0].shape[0]
    rows = lax.broadcasted_iota(jnp.int32, (rank, 2 * rank), 0)
    lanes = lax.broadcasted_iota(jnp.int32, (rank, 2 * rank), 1)
    eye = (
        lax.broadcasted_iota(jnp.int32, (rank, rank), 0)
        == lax.broadcasted_iota(jnp.int32, (rank, rank), 1)
    ).astype(F32)
    state = [jnp.concatenate([g, eye], axis=1) for g in grams]
    for j in range(rank - 1):
        below = rows > j
        for n, m in enumerate(state):
            column = jnp.broadcast_to(m[:, j : j + 1], m.shape)
            scaled = m[j : j + 1, :] / column[j : j + 1, :]
            state[n] = m - jnp.where(below, column, 0.0) * scaled
    out = []
    for m in state:
        diagonal = jnp.sum(jnp.where(rows == lanes, m, 0.0), axis=1, keepdims=True)
        m = m * lax.rsqrt(diagonal)
        upper = jnp.where((rows <= lanes)[:, :rank], m[:, :rank], 0.0)
        out.append((upper, m[:, rank:]))
    return out


def kernel(
    xs, local, u_hbm, v_hbm, sketch_hbm, diag_hbm, block_row, col_count, sample_out, gram_out, sums_out,
    sketch, diag, u_buf, v_buf, u_high, u_low, w_high, w_low, part, got_x, got_z, sample,
    gram, grams, group_gram, group_grams,
    load_sems, x_send, x_recv, z_send, z_recv, g_send, g_recv, r_send, r_recv, relay,
):
    slots, leaf_rows = u_buf.shape
    rank = sample.shape[0] // local
    blocks = slots // rank
    members = grams.shape[0]
    groups = group_grams.shape[0]
    zs = members // xs
    chunks = leaf_rows // WIDTH
    own_rows = local * rank
    me = lax.axis_index("dev")
    my_group = lax.axis_index("grp")
    z, x = me // xs, me % xs

    pairs = chunks // PAIR
    near_loads = [
        pltpu.make_async_copy(sketch_hbm, sketch, load_sems.at[0]),
        pltpu.make_async_copy(diag_hbm, diag, load_sems.at[1]),
    ]
    v_rows = slots // V_PARTS
    v_loads = [
        pltpu.make_async_copy(
            v_hbm.at[pl.ds(i * v_rows, v_rows)],
            v_buf.at[pl.ds(i * v_rows, v_rows)],
            load_sems.at[2 + i],
        )
        for i in range(V_PARTS)
    ]
    u_loads = []
    for p in range(pairs):
        at = pl.ds(p * PAIR * WIDTH, PAIR * WIDTH)
        u_loads.append(
            pltpu.make_async_copy(
                u_hbm.at[:, at], u_buf.at[:, at], load_sems.at[2 + V_PARTS + p]
            )
        )
    for load in near_loads[:1] + v_loads + u_loads + near_loads[1:]:
        load.start()
    barrier = pltpu.get_barrier_semaphore()
    for xo in range(1, xs):
        partner = z * xs + (x + xo) % xs
        pl.semaphore_signal(barrier, inc=1, device_id={"dev": partner}, device_id_type=MESH)
    for o in range(1, groups):
        pl.semaphore_signal(
            barrier, inc=1, device_id={"grp": (my_group + o) % groups}, device_id_type=MESH
        )

    def greet(semaphore):
        @pl.when(z > 0)
        def _():
            pl.semaphore_signal(
                semaphore, inc=1, device_id={"dev": me - xs}, device_id_type=MESH
            )

        @pl.when(z < zs - 1)
        def _():
            pl.semaphore_signal(
                semaphore, inc=1, device_id={"dev": me + xs}, device_id_type=MESH
            )

    half = zs // 2 if zs % 2 == 0 else zs
    side, step = z // half, z % half

    def peer_z(k):
        if k < half:
            return side * half + (step + k) % half
        return (1 - side) * half + (step + k - half) % half

    order = list(range(half, zs)) + list(range(1, half))
    near_z = jnp.where(z > 0, 1, 0) + jnp.where(z < zs - 1, 1, 0)
    greet(barrier)

    lane = lax.broadcasted_iota(jnp.int32, (1, slots), 1)
    row_of = jnp.zeros((1, slots), jnp.int32)
    slot_of = jnp.zeros((1, slots), jnp.int32)
    for s in range(blocks):
        row_of = jnp.where(lane >= s * rank, block_row[s], row_of)
        slot_of = jnp.where(lane >= s * rank, s, slot_of)
    col_of = jnp.zeros((1, slots), jnp.int32)
    end = 0
    for c in range(local):
        end = end + col_count[c]
        col_of = col_of + jnp.where(slot_of >= end, 1, 0)

    near_loads[0].wait()
    sketch_parts = split(sketch[...])
    parts = []
    for i in range(V_PARTS):
        v_loads[i].wait()
        parts.append(dot3(sketch_parts, split(v_buf[i * v_rows : (i + 1) * v_rows]), NT))
    every = jnp.concatenate(parts, axis=1)
    coupling = jnp.zeros((rank, slots), F32)
    for c in range(local):
        coupling = coupling + jnp.where(col_of == c, every[c * rank : (c + 1) * rank], 0.0)
    high, low = (part_.astype(F32) for part_ in split(coupling))

    def place(xo):
        for zo in range(zs):
            dest = peer_z(zo) * xs + (x + xo) % xs
            for c in range(local):
                hit = row_of == dest * local + c
                at = pl.ds((zo * local + c) * rank, rank)
                w_high[xo, at, :] = jnp.where(hit, high, 0.0).astype(BF16)
                w_low[xo, at, :] = jnp.where(hit, low, 0.0).astype(BF16)

    for xo in range(1, xs):
        place(xo)

    def contribute(xo, p):
        at = pl.ds(p * PAIR * WIDTH, PAIR * WIDTH)
        out = dot3((w_high[xo], w_low[xo]), (u_high[:, at], u_low[:, at]), NN)
        for h in range(PAIR):
            part[xo, p * PAIR + h] = out[:, h * WIDTH : (h + 1) * WIDTH]

    def x_copy(xo, q, k):
        at = pl.ds(k * own_rows, own_rows)
        return pltpu.make_async_remote_copy(
            src_ref=part.at[xo, q, at],
            dst_ref=got_x.at[xo - 1, q, at],
            send_sem=x_send.at[xo - 1, q, k],
            recv_sem=x_recv.at[xo - 1, q, k],
            device_id={"dev": z * xs + (x + xo) % xs},
            device_id_type=MESH,
        )

    def z_copy(zo, q):
        return pltpu.make_async_remote_copy(
            src_ref=part.at[0, q, pl.ds(zo * own_rows, own_rows)],
            dst_ref=got_z.at[zo - 1, q],
            send_sem=z_send.at[zo - 1, q],
            recv_sem=z_recv.at[zo - 1, q],
            device_id={"dev": peer_z(zo) * xs + x},
            device_id_type=MESH,
        )

    def pass_on(hop):
        pl.semaphore_wait(relay.at[hop], near_z)
        if hop < zs - 2:
            greet(relay.at[hop + 1])

    for p in range(pairs):
        at = pl.ds(p * PAIR * WIDTH, PAIR * WIDTH)
        u_loads[p].wait()
        u_high[:, at], u_low[:, at] = split(u_buf[:, at])
        for xo in range(1, xs):
            contribute(xo, p)
        if p == 0:
            pl.semaphore_wait(barrier, xs - 1 + groups - 1 + near_z)
            greet(relay.at[0])
        for q in range(p * PAIR, (p + 1) * PAIR):
            for k in order:
                for xo in range(1, xs):
                    x_copy(xo, q, k).start()
        if 1 <= p < zs:
            pass_on(p - 1)
    for q in range(chunks):
        for xo in range(1, xs):
            x_copy(xo, q, 0).start()
    for hop in range(min(pairs - 1, zs - 1), zs - 1):
        pass_on(hop)
    place(0)
    for p in range(pairs):
        contribute(0, p)
    for q in range(chunks):
        for k in order:
            at = pl.ds(k * own_rows, own_rows)
            total = part[0, q, at]
            for xo in range(1, xs):
                x_copy(xo, q, k).wait_recv()
                total = total + got_x[xo - 1, q, at]
            part[0, q, at] = total
            z_copy(k, q).start()
    near_loads[1].wait()
    leaf_gram = jnp.zeros((own_rows, own_rows), F32)
    for q in range(chunks):
        at = pl.ds(q * WIDTH, WIDTH)
        near = [
            diag[c : c + 1, at] * sketch[c * rank : (c + 1) * rank, at] for c in range(local)
        ]
        total = part[0, q, :own_rows] + jnp.concatenate(near, axis=0)
        for xo in range(1, xs):
            x_copy(xo, q, 0).wait_recv()
            total = total + got_x[xo - 1, q, :own_rows]
        for zo in range(1, zs):
            z_copy(zo, q).wait_recv()
            total = total + got_z[zo - 1, q]
        sample[:, at] = total
        leaf_gram = leaf_gram + dot(total, total, NT, HIGHEST)

    save = pltpu.make_async_copy(sample, sample_out, load_sems.at[0])
    save.start()
    gram_out[...] = leaf_gram
    packed = pack(
        functools.reduce(jnp.add, [diagonal_block(leaf_gram, c, rank) for c in range(local)])
    )
    gram[...] = packed
    grams[pl.ds(me, 1)] = packed[None]

    def g_copy(o):
        return pltpu.make_async_remote_copy(
            src_ref=gram,
            dst_ref=grams.at[me],
            send_sem=g_send.at[o - 1],
            recv_sem=g_recv.at[o - 1],
            device_id={"dev": (me + o) % members},
            device_id_type=MESH,
        )

    def r_copy(o):
        return pltpu.make_async_remote_copy(
            src_ref=group_gram,
            dst_ref=group_grams.at[my_group],
            send_sem=r_send.at[o - 1],
            recv_sem=r_recv.at[o - 1],
            device_id={"grp": (my_group + o) % groups},
            device_id_type=MESH,
        )

    for o in range(1, members):
        g_copy(o).start()
    for o in range(1, members):
        g_copy(o).wait_recv()
    packed_group = functools.reduce(jnp.add, [grams[i] for i in range(members)])
    group_gram[...] = packed_group
    group_grams[pl.ds(my_group, 1)] = packed_group[None]
    for o in range(1, groups):
        r_copy(o).start()
    for o in range(1, groups):
        r_copy(o).wait_recv()
    sums_out[0] = packed_group
    sums_out[1] = functools.reduce(jnp.add, [group_grams[i] for i in range(groups)])

    for q in range(chunks):
        for xo in range(1, xs):
            for k in range(zs):
                x_copy(xo, q, k).wait_send()
        for zo in range(1, zs):
            z_copy(zo, q).wait_send()
    for o in range(1, members):
        g_copy(o).wait_send()
    for o in range(1, groups):
        r_copy(o).wait_send()
    save.wait()


def finish(members, groups, sample_hbm, leaf_gram, sums, basis, t_leaf, t_group, sample, load_sem):
    local, rank, leaf_rows = basis.shape
    load = pltpu.make_async_copy(sample_hbm, sample, load_sem)
    load.start()
    whole = leaf_gram[...]
    squares = [diagonal_block(whole, c, rank) for c in range(local)]
    factors = factor(squares + [unpack(sums[0], rank), unpack(sums[1], rank)])
    leaves, (group_upper, group_inverse), (_, root_inverse) = factors[:local], *factors[local:]
    for c in range(local):
        t_leaf[c] = dot(leaves[c][0], group_inverse, NT, HIGHEST) * math.sqrt(members * local)
    t_group[0] = dot(group_upper, root_inverse, NT, HIGHEST) * math.sqrt(groups)
    load.wait()
    for c in range(local):
        basis[c] = dot(
            leaves[c][1] * math.sqrt(leaf_rows), sample[c * rank : (c + 1) * rank], NN, HIGHEST
        )


def body(u_blocks, v_blocks, sketch, near_diag, block_row, col_count):
    blocks, rank, leaf_rows = u_blocks.shape
    local = sketch.shape[0]
    members = lax.axis_size("dev")
    groups = lax.axis_size("grp")
    xs = max(d for d in range(1, members + 1) if members % d == 0 and d * d <= members)
    zs = members // xs
    chunks = leaf_rows // WIDTH
    slots = blocks * rank
    own = local * rank
    vmem = pl.BlockSpec(memory_space=pltpu.VMEM)
    smem = pl.BlockSpec(memory_space=pltpu.SMEM)
    hbm = pl.BlockSpec(memory_space=pl.ANY)
    dma = pltpu.SemaphoreType.DMA
    sample, leaf_gram, sums = pl.pallas_call(
        functools.partial(kernel, xs, local),
        out_shape=(
            jax.ShapeDtypeStruct((own, leaf_rows), F32),
            jax.ShapeDtypeStruct((own, own), F32),
            jax.ShapeDtypeStruct((2, 8, rank * rank // 8), F32),
        ),
        in_specs=[hbm, hbm, hbm, hbm, smem, smem],
        out_specs=(hbm, vmem, vmem),
        scratch_shapes=[
            pltpu.VMEM((own, leaf_rows), F32),
            pltpu.VMEM((local, leaf_rows), F32),
            pltpu.VMEM((slots, leaf_rows), F32),
            pltpu.VMEM((slots, leaf_rows), F32),
            pltpu.VMEM((slots, leaf_rows), BF16),
            pltpu.VMEM((slots, leaf_rows), BF16),
            pltpu.VMEM((xs, zs * own, slots), BF16),
            pltpu.VMEM((xs, zs * own, slots), BF16),
            pltpu.VMEM((xs, chunks, zs * own, WIDTH), F32),
            pltpu.VMEM((max(xs - 1, 1), chunks, zs * own, WIDTH), F32),
            pltpu.VMEM((max(zs - 1, 1), chunks, own, WIDTH), F32),
            pltpu.VMEM((own, leaf_rows), F32),
            pltpu.VMEM((8, rank * rank // 8), F32),
            pltpu.VMEM((members, 8, rank * rank // 8), F32),
            pltpu.VMEM((8, rank * rank // 8), F32),
            pltpu.VMEM((groups, 8, rank * rank // 8), F32),
            dma((2 + V_PARTS + chunks // PAIR,)),
            dma((max(xs - 1, 1), chunks, zs)),
            dma((max(xs - 1, 1), chunks, zs)),
            dma((max(zs - 1, 1), chunks)),
            dma((max(zs - 1, 1), chunks)),
            dma((members - 1,)),
            dma((members - 1,)),
            dma((groups - 1,)),
            dma((groups - 1,)),
            pltpu.SemaphoreType.REGULAR((max(zs - 1, 1),)),
        ],
        compiler_params=pltpu.CompilerParams(
            collective_id=0, has_side_effects=True, vmem_limit_bytes=60 * 1024 * 1024
        ),
    )(
        u_blocks.reshape(slots, leaf_rows),
        v_blocks.reshape(slots, leaf_rows),
        sketch.reshape(own, leaf_rows),
        near_diag,
        block_row,
        col_count,
    )
    return pl.pallas_call(
        functools.partial(finish, members, groups),
        out_shape=(
            jax.ShapeDtypeStruct((local, rank, leaf_rows), F32),
            jax.ShapeDtypeStruct((local, rank, rank), F32),
            jax.ShapeDtypeStruct((1, rank, rank), F32),
        ),
        in_specs=[hbm, vmem, vmem],
        out_specs=(vmem, vmem, vmem),
        scratch_shapes=[pltpu.VMEM((own, leaf_rows), F32), dma],
    )(sample, leaf_gram, sums)


def solution(mesh):
    in_specs = (
        P(("grp", "dev"), None, None),
        P(("grp", "dev"), None, None),
        P(("grp", "dev"), None, None),
        P(("grp", "dev"), None),
        P(("grp", "dev")),
        P(("grp", "dev")),
    )
    out_specs = (P(("grp", "dev"), None, None), P(("grp", "dev"), None, None), P("grp", None, None))
    return jax.shard_map(body, mesh=mesh, in_specs=in_specs, out_specs=out_specs, check_vma=False)
```

profile of v0, /device:TPU:0, one launch (start us, length us, event | category | flops | bytes accessed | tf_op | source)
XLA Modules:
  0.0 52.1 jit_solution(6753211102570089356)
XLA Ops:
  0.6 46.6 %shard_map.85 = (f32[64,1024]{1,0:T(8,128)}, f32[64,64]{1,0:T(8,128)}, f32[2,8,128]{2,1,0:T(8,128)}) custom-call(f32[768,1024]{1,0:T(8,128)} %bitcast.3, f32[768,1024]{1,0:T(8,128)} %bitcast.4, f32[64,1024]{1,0:T(8,128)} %bitcast.5, f32[2,1024]{1,0:T(2,128)} %diag_hbm.1, s32[24]{0:T(128)} %block_row.1, s32[2]{0:T(128)} %col_count.1), custom_call_target="tpu_custom_call" | custom-call | tf_op jit(solution)/shard_map/pallas_call | solution.py:355
  47.2 4.9 %shard_map.86 = (f32[2,32,1024]{2,1,0:T(8,128)}, f32[2,32,32]{2,1,0:T(8,128)}, f32[1,32,32]{2,1,0:T(8,128)}) custom-call(f32[64,1024]{1,0:T(8,128)} %get-tuple-element.6.sample_hbm, f32[64,64]{1,0:T(8,128)} %get-tuple-element.7.leaf_gram, f32[2,8,128]{2,1,0:T(8,128)} %get-tuple-element.8.sums), custom_call_target="tpu_custom_call" | custom-call | tf_op jit(solution)/shard_map/pallas_call | solution.py:403
where the time goes:
time: 52.3 us; the launch traced here: 52.1 us
  Pallas kernels  51.5 us (98%)
  between operations  0.64 us (1%)
    pallas_call x1, Pallas kernels, body(): pl.pallas_call(functools.partial(kernel, xs, local), out_shape=(jax.Shape...  46.6 us
    pallas_call x1, Pallas kernels, body(): pl.pallas_call(functools.partial(finish, members, groups), out_shape=(jax...  4.91 us

commit v1 on v0

--- a/solution.py
+++ b/solution.py
@@ -73,9 +73,9 @@
 
 def kernel(
     xs, local, u_hbm, v_hbm, sketch_hbm, diag_hbm, block_row, col_count, sample_out, gram_out, sums_out,
-    sketch, diag, u_buf, v_buf, u_high, u_low, w_high, w_low, part, got_x, got_z, sample,
+    sketch, diag, u_buf, v_buf, u_high, u_low, w_high, w_low, part, got_x, got_mate, got_far, sample,
     gram, grams, group_gram, group_grams,
-    load_sems, x_send, x_recv, z_send, z_recv, g_send, g_recv, r_send, r_recv, relay,
+    load_sems, x_send, x_recv, m_send, m_recv, f_send, f_recv, g_send, g_recv, r_send, r_recv, relay,
 ):
     slots, leaf_rows = u_buf.shape
     rank = sample.shape[0] // local
@@ -135,15 +135,18 @@
                 semaphore, inc=1, device_id={"dev": me + xs}, device_id_type=MESH
             )
 
-    half = zs // 2 if zs % 2 == 0 else zs
-    side, step = z // half, z % half
+    team = 2 if zs % 2 == 0 else 1
+    first, seat = z // team * team, z % team
+    teams = zs // team
 
     def peer_z(k):
-        if k < half:
-            return side * half + (step + k) % half
-        return (1 - side) * half + (step + k - half) % half
-
-    order = list(range(half, zs)) + list(range(1, half))
+        if k == 0:
+            return z
+        if k < team:
+            return first + (seat + k) % team
+        return (first + k) % zs
+
+    order = list(range(team, zs)) + list(range(1, team))
     near_z = jnp.where(z > 0, 1, 0) + jnp.where(z < zs - 1, 1, 0)
     greet(barrier)
 
@@ -200,15 +203,32 @@
             device_id_type=MESH,
         )
 
-    def z_copy(zo, q):
+    def block(k):
+        return pl.ds(k * own_rows, own_rows)
+
+    def mate_copy(k, q):
         return pltpu.make_async_remote_copy(
-            src_ref=part.at[0, q, pl.ds(zo * own_rows, own_rows)],
-            dst_ref=got_z.at[zo - 1, q],
-            send_sem=z_send.at[zo - 1, q],
-            recv_sem=z_recv.at[zo - 1, q],
-            device_id={"dev": peer_z(zo) * xs + x},
+            src_ref=part.at[0, q, block(k)],
+            dst_ref=got_mate.at[k - 1, q],
+            send_sem=m_send.at[k - 1, q],
+            recv_sem=m_recv.at[k - 1, q],
+            device_id={"dev": (first + team - 1 - seat) * xs + x},
             device_id_type=MESH,
         )
+
+    def far_copy(k, q):
+        slot = teams - k // team - 1
+        return pltpu.make_async_remote_copy(
+            src_ref=part.at[0, q, block(k)],
+            dst_ref=got_far.at[slot, q],
+            send_sem=f_send.at[k - team, q],
+            recv_sem=f_recv.at[slot, q],
+            device_id={"dev": peer_z(k) * xs + x},
+            device_id_type=MESH,
+        )
+
+    def hands_over(k):
+        return jnp.where(first + k < zs, 0, 1) == seat
 
     def pass_on(hop):
         pl.semaphore_wait(relay.at[hop], near_z)
@@ -236,17 +256,36 @@
     for hop in range(min(pairs - 1, zs - 1), zs - 1):
         pass_on(hop)
     place(0)
+
+    def gather(k, q):
+        total = part[0, q, block(k)]
+        for xo in range(1, xs):
+            x_copy(xo, q, k).wait_recv()
+            total = total + got_x[xo - 1, q, block(k)]
+        return total
+
     for p in range(pairs):
         contribute(0, p)
-    for q in range(chunks):
-        for k in order:
-            at = pl.ds(k * own_rows, own_rows)
-            total = part[0, q, at]
-            for xo in range(1, xs):
-                x_copy(xo, q, k).wait_recv()
-                total = total + got_x[xo - 1, q, at]
-            part[0, q, at] = total
-            z_copy(k, q).start()
+        for q in range(p * PAIR, (p + 1) * PAIR):
+            for k in order:
+                part[0, q, block(k)] = gather(k, q)
+                if k < team:
+                    mate_copy(k, q).start()
+                elif team > 1:
+                    @pl.when(hands_over(k))
+                    def _(k=k, q=q):
+                        mate_copy(k, q).start()
+            for k in range(team, zs):
+                def send_far(k=k, q=q):
+                    if team > 1:
+                        mate_copy(k, q).wait_recv()
+                        part[0, q, block(k)] = part[0, q, block(k)] + got_mate[k - 1, q]
+                    far_copy(k, q).start()
+
+                if team > 1:
+                    pl.when(jnp.logical_not(hands_over(k)))(send_far)
+                else:
+                    send_far()
     near_loads[1].wait()
     leaf_gram = jnp.zeros((own_rows, own_rows), F32)
     for q in range(chunks):
@@ -254,13 +293,14 @@
         near = [
             diag[c : c + 1, at] * sketch[c * rank : (c + 1) * rank, at] for c in range(local)
         ]
-        total = part[0, q, :own_rows] + jnp.concatenate(near, axis=0)
-        for xo in range(1, xs):
-            x_copy(xo, q, 0).wait_recv()
-            total = total + got_x[xo - 1, q, :own_rows]
-        for zo in range(1, zs):
-            z_copy(zo, q).wait_recv()
-            total = total + got_z[zo - 1, q]
+        total = gather(0, q) + jnp.concatenate(near, axis=0)
+        for k in range(1, team):
+            mate_copy(k, q).wait_recv()
+            total = total + got_mate[k - 1, q]
+        for k in range(team, zs, team):
+            slot = teams - k // team - 1
+            far_copy(k, q).wait_recv()
+            total = total + got_far[slot, q]
         sample[:, at] = total
         leaf_gram = leaf_gram + dot(total, total, NT, HIGHEST)
 
@@ -311,8 +351,17 @@
         for xo in range(1, xs):
             for k in range(zs):
                 x_copy(xo, q, k).wait_send()
-        for zo in range(1, zs):
-            z_copy(zo, q).wait_send()
+        for k in range(1, team):
+            mate_copy(k, q).wait_send()
+        for k in range(team, zs):
+            def sent(copy, k=k, q=q):
+                copy(k, q).wait_send()
+
+            if team > 1:
+                pl.when(hands_over(k))(functools.partial(sent, mate_copy))
+                pl.when(jnp.logical_not(hands_over(k)))(functools.partial(sent, far_copy))
+            else:
+                sent(far_copy)
     for o in range(1, members):
         g_copy(o).wait_send()
     for o in range(1, groups):
@@ -345,6 +394,7 @@
     groups = lax.axis_size("grp")
     xs = max(d for d in range(1, members + 1) if members % d == 0 and d * d <= members)
     zs = members // xs
+    team = 2 if zs % 2 == 0 else 1
     chunks = leaf_rows // WIDTH
     slots = blocks * rank
     own = local * rank
@@ -373,6 +423,7 @@
             pltpu.VMEM((xs, chunks, zs * own, WIDTH), F32),
             pltpu.VMEM((max(xs - 1, 1), chunks, zs * own, WIDTH), F32),
             pltpu.VMEM((max(zs - 1, 1), chunks, own, WIDTH), F32),
+            pltpu.VMEM((max(zs // team - 1, 1), chunks, own, WIDTH), F32),
             pltpu.VMEM((own, leaf_rows), F32),
             pltpu.VMEM((8, rank * rank // 8), F32),
             pltpu.VMEM((members, 8, rank * rank // 8), F32),
@@ -383,6 +434,8 @@
             dma((max(xs - 1, 1), chunks, zs)),
             dma((max(zs - 1, 1), chunks)),
             dma((max(zs - 1, 1), chunks)),
+            dma((max(zs - team, 1), chunks)),
+            dma((max(zs // team - 1, 1), chunks)),
             dma((members - 1,)),
             dma((members - 1,)),
             dma((groups - 1,)),

time: 52.3 us -> 49.1 us (0.939)
  Pallas kernels: 51.5 us -> 48.2 us
    pallas_call x1, Pallas kernels: 46.6 us -> 43.3 us  [body(): pl.pallas_call(functools.partial(kernel, xs, local), out_shape=(jax.Shape...]
where the time goes in v1:
time: 49.1 us; the launch traced here: 48.9 us
  Pallas kernels  48.2 us (98%)
  between operations  0.64 us (1%)
    pallas_call x1, Pallas kernels, body(): pl.pallas_call(functools.partial(kernel, xs, local), out_shape=(jax.Shape...  43.3 us
    pallas_call x1, Pallas kernels, body(): pl.pallas_call(functools.partial(finish, members, groups), out_shape=(jax...  4.91 us

profile of v1, /device:TPU:0, one launch (start us, length us, event | category | flops | bytes accessed | tf_op | source)
XLA Modules:
  0.0 48.9 jit_solution(10220367595439319222)
XLA Ops:
  0.6 43.3 %shard_map.85 = (f32[64,1024]{1,0:T(8,128)}, f32[64,64]{1,0:T(8,128)}, f32[2,8,128]{2,1,0:T(8,128)}) custom-call(f32[768,1024]{1,0:T(8,128)} %bitcast.3, f32[768,1024]{1,0:T(8,128)} %bitcast.4, f32[64,1024]{1,0:T(8,128)} %bitcast.5, f32[2,1024]{1,0:T(2,128)} %diag_hbm.1, s32[24]{0:T(128)} %block_row.1, s32[2]{0:T(128)} %col_count.1), custom_call_target="tpu_custom_call" | custom-call | tf_op jit(solution)/shard_map/pallas_call | solution.py:405
  44.0 4.9 %shard_map.86 = (f32[2,32,1024]{2,1,0:T(8,128)}, f32[2,32,32]{2,1,0:T(8,128)}, f32[1,32,32]{2,1,0:T(8,128)}) custom-call(f32[64,1024]{1,0:T(8,128)} %get-tuple-element.6.sample_hbm, f32[64,64]{1,0:T(8,128)} %get-tuple-element.7.leaf_gram, f32[2,8,128]{2,1,0:T(8,128)} %get-tuple-element.8.sums), custom_call_target="tpu_custom_call" | custom-call | tf_op jit(solution)/shard_map/pallas_call | solution.py:456

commit v2 on v1

--- a/solution.py
+++ b/solution.py
@@ -17,6 +17,7 @@
 WIDTH = 128
 PAIR = 2
 V_PARTS = 3
+PIVOTS = 8
 
 
 def dot(a, b, dims, precision=None):
@@ -56,12 +57,19 @@
         == lax.broadcasted_iota(jnp.int32, (rank, rank), 1)
     ).astype(F32)
     state = [jnp.concatenate([g, eye], axis=1) for g in grams]
-    for j in range(rank - 1):
-        below = rows > j
-        for n, m in enumerate(state):
-            column = jnp.broadcast_to(m[:, j : j + 1], m.shape)
-            scaled = m[j : j + 1, :] / column[j : j + 1, :]
-            state[n] = m - jnp.where(below, column, 0.0) * scaled
+    for j in range(0, rank, PIVOTS):
+        ahead = [
+            [jnp.broadcast_to(m[:, j + b : j + b + 1], m.shape) for b in range(PIVOTS)] for m in state
+        ]
+        for b in range(min(PIVOTS, rank - 1 - j)):
+            below = rows > j + b
+            for n, m in enumerate(state):
+                column = ahead[n][b]
+                inverse = 1.0 / column[j + b : j + b + 1]
+                low = jnp.where(below, column, 0.0)
+                state[n] = m - low * (m[j + b : j + b + 1] * inverse)
+                for e in range(b + 1, PIVOTS):
+                    ahead[n][e] = ahead[n][e] - low * (column[j + e : j + e + 1] * inverse)
     out = []
     for m in state:
         diagonal = jnp.sum(jnp.where(rows == lanes, m, 0.0), axis=1, keepdims=True)
@@ -71,10 +79,19 @@
     return out
 
 
+def pieces_of(chunks):
+    starts = list(range(0, chunks, PAIR))
+    return [range(a, b) for a, b in zip(starts, starts[1:] + [chunks])]
+
+
+def columns(piece):
+    return pl.ds(piece.start * WIDTH, len(piece) * WIDTH)
+
+
 def kernel(
-    xs, local, u_hbm, v_hbm, sketch_hbm, diag_hbm, block_row, col_count, sample_out, gram_out, sums_out,
-    sketch, diag, u_buf, v_buf, u_high, u_low, w_high, w_low, part, got_x, got_mate, got_far, sample,
-    gram, grams, group_gram, group_grams,
+    xs, local, u_hbm, v_hbm, sketch_hbm, diag_hbm, row_hbm, count_hbm, sample_out, squares_out,
+    block_row, col_count, sketch, diag, u_buf, v_buf, u_high, u_low, w_high, w_low, part, got_x, got_mate, got_far, sample,
+    gram, grams, group_gram, group_grams, uppers,
     load_sems, x_send, x_recv, m_send, m_recv, f_send, f_recv, g_send, g_recv, r_send, r_recv, relay,
 ):
     slots, leaf_rows = u_buf.shape
@@ -89,7 +106,7 @@
     my_group = lax.axis_index("grp")
     z, x = me // xs, me % xs
 
-    pairs = chunks // PAIR
+    pieces = pieces_of(chunks)
     near_loads = [
         pltpu.make_async_copy(sketch_hbm, sketch, load_sems.at[0]),
         pltpu.make_async_copy(diag_hbm, diag, load_sems.at[1]),
@@ -104,14 +121,18 @@
         for i in range(V_PARTS)
     ]
     u_loads = []
-    for p in range(pairs):
-        at = pl.ds(p * PAIR * WIDTH, PAIR * WIDTH)
+    for p, piece in enumerate(pieces):
+        at = columns(piece)
         u_loads.append(
             pltpu.make_async_copy(
-                u_hbm.at[:, at], u_buf.at[:, at], load_sems.at[2 + V_PARTS + p]
+                u_hbm.at[:, at], u_buf.at[:, at], load_sems.at[4 + V_PARTS + p]
             )
         )
-    for load in near_loads[:1] + v_loads + u_loads + near_loads[1:]:
+    index_loads = [
+        pltpu.make_async_copy(row_hbm, block_row, load_sems.at[2 + V_PARTS]),
+        pltpu.make_async_copy(count_hbm, col_count, load_sems.at[3 + V_PARTS]),
+    ]
+    for load in index_loads + near_loads[:1] + v_loads + u_loads + near_loads[1:]:
         load.start()
     barrier = pltpu.get_barrier_semaphore()
     for xo in range(1, xs):
@@ -150,6 +171,8 @@
     near_z = jnp.where(z > 0, 1, 0) + jnp.where(z < zs - 1, 1, 0)
     greet(barrier)
 
+    for load in index_loads:
+        load.wait()
     lane = lax.broadcasted_iota(jnp.int32, (1, slots), 1)
     row_of = jnp.zeros((1, slots), jnp.int32)
     slot_of = jnp.zeros((1, slots), jnp.int32)
@@ -186,11 +209,11 @@
     for xo in range(1, xs):
         place(xo)
 
-    def contribute(xo, p):
-        at = pl.ds(p * PAIR * WIDTH, PAIR * WIDTH)
+    def contribute(xo, piece):
+        at = columns(piece)
         out = dot3((w_high[xo], w_low[xo]), (u_high[:, at], u_low[:, at]), NN)
-        for h in range(PAIR):
-            part[xo, p * PAIR + h] = out[:, h * WIDTH : (h + 1) * WIDTH]
+        for h, q in enumerate(piece):
+            part[xo, q] = out[:, h * WIDTH : (h + 1) * WIDTH]
 
     def x_copy(xo, q, k):
         at = pl.ds(k * own_rows, own_rows)
@@ -235,25 +258,23 @@
         if hop < zs - 2:
             greet(relay.at[hop + 1])
 
-    for p in range(pairs):
-        at = pl.ds(p * PAIR * WIDTH, PAIR * WIDTH)
+    for p, piece in enumerate(pieces):
+        at = columns(piece)
         u_loads[p].wait()
         u_high[:, at], u_low[:, at] = split(u_buf[:, at])
         for xo in range(1, xs):
-            contribute(xo, p)
+            contribute(xo, piece)
         if p == 0:
             pl.semaphore_wait(barrier, xs - 1 + groups - 1 + near_z)
             greet(relay.at[0])
-        for q in range(p * PAIR, (p + 1) * PAIR):
+        for q in piece:
             for k in order:
                 for xo in range(1, xs):
                     x_copy(xo, q, k).start()
-        if 1 <= p < zs:
-            pass_on(p - 1)
     for q in range(chunks):
         for xo in range(1, xs):
             x_copy(xo, q, 0).start()
-    for hop in range(min(pairs - 1, zs - 1), zs - 1):
+    for hop in range(zs - 1):
         pass_on(hop)
     place(0)
 
@@ -264,9 +285,9 @@
             total = total + got_x[xo - 1, q, block(k)]
         return total
 
-    for p in range(pairs):
-        contribute(0, p)
-        for q in range(p * PAIR, (p + 1) * PAIR):
+    for piece in pieces:
+        contribute(0, piece)
+        for q in piece:
             for k in order:
                 part[0, q, block(k)] = gather(k, q)
                 if k < team:
@@ -306,10 +327,8 @@
 
     save = pltpu.make_async_copy(sample, sample_out, load_sems.at[0])
     save.start()
-    gram_out[...] = leaf_gram
-    packed = pack(
-        functools.reduce(jnp.add, [diagonal_block(leaf_gram, c, rank) for c in range(local)])
-    )
+    squares = [diagonal_block(leaf_gram, c, rank) for c in range(local)]
+    packed = pack(functools.reduce(jnp.add, squares))
     gram[...] = packed
     grams[pl.ds(me, 1)] = packed[None]
 
@@ -335,6 +354,13 @@
 
     for o in range(1, members):
         g_copy(o).start()
+
+    @pl.when(me < members)
+    def _():
+        for c, (upper, inverse) in enumerate(factor(squares)):
+            uppers[c] = upper
+            squares_out[local + c] = inverse * math.sqrt(leaf_rows)
+
     for o in range(1, members):
         g_copy(o).wait_recv()
     packed_group = functools.reduce(jnp.add, [grams[i] for i in range(members)])
@@ -342,10 +368,18 @@
     group_grams[pl.ds(my_group, 1)] = packed_group[None]
     for o in range(1, groups):
         r_copy(o).start()
+
+    @pl.when(my_group < groups)
+    def _():
+        ((upper, inverse),) = factor([unpack(packed_group, rank)])
+        for c in range(local):
+            squares_out[c] = dot(uppers[c], inverse, NT, HIGHEST) * math.sqrt(members * local)
+        squares_out[2 * local] = upper * math.sqrt(groups)
+
     for o in range(1, groups):
         r_copy(o).wait_recv()
-    sums_out[0] = packed_group
-    sums_out[1] = functools.reduce(jnp.add, [group_grams[i] for i in range(groups)])
+    packed_root = functools.reduce(jnp.add, [group_grams[i] for i in range(groups)])
+    squares_out[2 * local + 1] = unpack(packed_root, rank)
 
     for q in range(chunks):
         for xo in range(1, xs):
@@ -369,22 +403,17 @@
     save.wait()
 
 
-def finish(members, groups, sample_hbm, leaf_gram, sums, basis, t_leaf, t_group, sample, load_sem):
-    local, rank, leaf_rows = basis.shape
+def finish(sample_hbm, squares, basis, t_leaf, t_group, sample, load_sem):
+    local, rank, _ = basis.shape
     load = pltpu.make_async_copy(sample_hbm, sample, load_sem)
     load.start()
-    whole = leaf_gram[...]
-    squares = [diagonal_block(whole, c, rank) for c in range(local)]
-    factors = factor(squares + [unpack(sums[0], rank), unpack(sums[1], rank)])
-    leaves, (group_upper, group_inverse), (_, root_inverse) = factors[:local], *factors[local:]
     for c in range(local):
-        t_leaf[c] = dot(leaves[c][0], group_inverse, NT, HIGHEST) * math.sqrt(members * local)
-    t_group[0] = dot(group_upper, root_inverse, NT, HIGHEST) * math.sqrt(groups)
+        t_leaf[c] = squares[c]
+    ((_, root_inverse),) = factor([squares[2 * local + 1]])
+    t_group[0] = dot(squares[2 * local], root_inverse, NT, HIGHEST)
     load.wait()
     for c in range(local):
-        basis[c] = dot(
-            leaves[c][1] * math.sqrt(leaf_rows), sample[c * rank : (c + 1) * rank], NN, HIGHEST
-        )
+        basis[c] = dot(squares[local + c], sample[c * rank : (c + 1) * rank], NN, HIGHEST)
 
 
 def body(u_blocks, v_blocks, sketch, near_diag, block_row, col_count):
@@ -399,19 +428,19 @@
     slots = blocks * rank
     own = local * rank
     vmem = pl.BlockSpec(memory_space=pltpu.VMEM)
-    smem = pl.BlockSpec(memory_space=pltpu.SMEM)
     hbm = pl.BlockSpec(memory_space=pl.ANY)
     dma = pltpu.SemaphoreType.DMA
-    sample, leaf_gram, sums = pl.pallas_call(
+    sample, squares = pl.pallas_call(
         functools.partial(kernel, xs, local),
         out_shape=(
             jax.ShapeDtypeStruct((own, leaf_rows), F32),
-            jax.ShapeDtypeStruct((own, own), F32),
-            jax.ShapeDtypeStruct((2, 8, rank * rank // 8), F32),
+            jax.ShapeDtypeStruct((2 * local + 2, rank, rank), F32),
         ),
-        in_specs=[hbm, hbm, hbm, hbm, smem, smem],
-        out_specs=(hbm, vmem, vmem),
+        in_specs=[hbm] * 6,
+        out_specs=(hbm, vmem),
         scratch_shapes=[
+            pltpu.SMEM((blocks,), jnp.int32),
+            pltpu.SMEM((local,), jnp.int32),
             pltpu.VMEM((own, leaf_rows), F32),
             pltpu.VMEM((local, leaf_rows), F32),
             pltpu.VMEM((slots, leaf_rows), F32),
@@ -429,7 +458,8 @@
             pltpu.VMEM((members, 8, rank * rank // 8), F32),
             pltpu.VMEM((8, rank * rank // 8), F32),
             pltpu.VMEM((groups, 8, rank * rank // 8), F32),
-            dma((2 + V_PARTS + chunks // PAIR,)),
+            pltpu.VMEM((local, rank, rank), F32),
+            dma((4 + V_PARTS + len(pieces_of(chunks)),)),
             dma((max(xs - 1, 1), chunks, zs)),
             dma((max(xs - 1, 1), chunks, zs)),
             dma((max(zs - 1, 1), chunks)),
@@ -454,16 +484,16 @@
         col_count,
     )
     return pl.pallas_call(
-        functools.partial(finish, members, groups),
+        finish,
         out_shape=(
             jax.ShapeDtypeStruct((local, rank, leaf_rows), F32),
             jax.ShapeDtypeStruct((local, rank, rank), F32),
             jax.ShapeDtypeStruct((1, rank, rank), F32),
         ),
-        in_specs=[hbm, vmem, vmem],
+        in_specs=[hbm, vmem],
         out_specs=(vmem, vmem, vmem),
         scratch_shapes=[pltpu.VMEM((own, leaf_rows), F32), dma],
-    )(sample, leaf_gram, sums)
+    )(sample, squares)
 
 
 def solution(mesh):

time: 49.1 us -> 47.7 us (0.971)
  Pallas kernels: 48.2 us -> 46.9 us
    pallas_call x1, Pallas kernels: 4.91 us -> 3.01 us  [body(): pl.pallas_call(finish, out_shape=(jax.ShapeDtypeStruct((local, rank, leaf...]
    pallas_call x1, Pallas kernels: 43.3 us -> 43.9 us  [body(): pl.pallas_call(functools.partial(kernel, xs, local), out_shape=(jax.Shape...]
where the time goes in v2:
time: 47.7 us; the launch traced here: 47.6 us
  Pallas kernels  46.9 us (98%)
  between operations  0.64 us (1%)
    pallas_call x1, Pallas kernels, body(): pl.pallas_call(functools.partial(kernel, xs, local), out_shape=(jax.Shape...  43.9 us
    pallas_call x1, Pallas kernels, body(): pl.pallas_call(finish, out_shape=(jax.ShapeDtypeStruct((local, rank, leaf...  3.01 us

profile of v2, /device:TPU:0, one launch (start us, length us, event | category | flops | bytes accessed | tf_op | source)
XLA Modules:
  0.0 47.6 jit_solution(12772225878240358173)
XLA Ops:
  0.6 43.9 %shard_map.85 = (f32[64,1024]{1,0:T(8,128)}, f32[6,32,32]{2,1,0:T(8,128)}) custom-call(f32[768,1024]{1,0:T(8,128)} %bitcast.3, f32[768,1024]{1,0:T(8,128)} %bitcast.4, f32[64,1024]{1,0:T(8,128)} %bitcast.5, f32[2,1024]{1,0:T(2,128)} %diag_hbm.1, s32[24]{0:T(128)} %row_hbm.1, s32[2]{0:T(128)} %count_hbm.1), custom_call_target="tpu_custom_call" | custom-call | tf_op jit(solution)/shard_map/pallas_call | solution.py:433
  44.6 3.0 %shard_map.86 = (f32[2,32,1024]{2,1,0:T(8,128)}, f32[2,32,32]{2,1,0:T(8,128)}, f32[1,32,32]{2,1,0:T(8,128)}) custom-call(f32[64,1024]{1,0:T(8,128)} %get-tuple-element.5.sample_hbm, f32[6,32,32]{2,1,0:T(8,128)} %get-tuple-element.6.squares), custom_call_target="tpu_custom_call" | custom-call | tf_op jit(solution)/shard_map/pallas_call | solution.py:486

commit v3 on v2

--- a/solution.py
+++ b/solution.py
@@ -79,9 +79,13 @@
     return out
 
 
-def pieces_of(chunks):
-    starts = list(range(0, chunks, PAIR))
+def pieces_of(chunks, early):
+    starts = list(range(early, chunks, PAIR))
     return [range(a, b) for a, b in zip(starts, starts[1:] + [chunks])]
+
+
+def early_of(chunks, xs, zs):
+    return chunks // 8 if xs > 1 and zs > 2 and zs % 2 == 0 else 0
 
 
 def columns(piece):
@@ -106,7 +110,10 @@
     my_group = lax.axis_index("grp")
     z, x = me // xs, me % xs
 
-    pieces = pieces_of(chunks)
+    early = early_of(chunks, xs, zs)
+    pieces = pieces_of(chunks, early)
+    loads = pieces + ([range(early)] if early else [])
+    loads = loads[:1] + loads[len(pieces) :] + loads[1 : len(pieces)]
     near_loads = [
         pltpu.make_async_copy(sketch_hbm, sketch, load_sems.at[0]),
         pltpu.make_async_copy(diag_hbm, diag, load_sems.at[1]),
@@ -121,7 +128,7 @@
         for i in range(V_PARTS)
     ]
     u_loads = []
-    for p, piece in enumerate(pieces):
+    for p, piece in enumerate(loads):
         at = columns(piece)
         u_loads.append(
             pltpu.make_async_copy(
@@ -229,23 +236,26 @@
     def block(k):
         return pl.ds(k * own_rows, own_rows)
 
-    def mate_copy(k, q):
+    def lane_of(q, xo):
+        return q if xo == 0 else chunks + (xo - 1) * early + q
+
+    def mate_copy(k, q, xo=0):
         return pltpu.make_async_remote_copy(
-            src_ref=part.at[0, q, block(k)],
-            dst_ref=got_mate.at[k - 1, q],
-            send_sem=m_send.at[k - 1, q],
-            recv_sem=m_recv.at[k - 1, q],
+            src_ref=part.at[xo, q, block(k)],
+            dst_ref=got_mate.at[k - 1, lane_of(q, xo)],
+            send_sem=m_send.at[k - 1, lane_of(q, xo)],
+            recv_sem=m_recv.at[k - 1, lane_of(q, xo)],
             device_id={"dev": (first + team - 1 - seat) * xs + x},
             device_id_type=MESH,
         )
 
-    def far_copy(k, q):
+    def far_copy(k, q, xo=0):
         slot = teams - k // team - 1
         return pltpu.make_async_remote_copy(
-            src_ref=part.at[0, q, block(k)],
-            dst_ref=got_far.at[slot, q],
-            send_sem=f_send.at[k - team, q],
-            recv_sem=f_recv.at[slot, q],
+            src_ref=part.at[xo, q, block(k)],
+            dst_ref=got_far.at[slot, lane_of(q, xo)],
+            send_sem=f_send.at[k - team, lane_of(q, xo)],
+            recv_sem=f_recv.at[slot, lane_of(q, xo)],
             device_id={"dev": peer_z(k) * xs + x},
             device_id_type=MESH,
         )
@@ -258,10 +268,60 @@
         if hop < zs - 2:
             greet(relay.at[hop + 1])
 
+    def gather(k, q):
+        total = part[0, q, block(k)]
+        for xo in range(1, xs):
+            x_copy(xo, q, k).wait_recv()
+            total = total + got_x[xo - 1, q, block(k)]
+        return total
+
+    def to_mate(k, q, xo):
+        if k < team:
+            mate_copy(k, q, xo).start()
+        elif team > 1:
+            @pl.when(hands_over(k))
+            def _():
+                mate_copy(k, q, xo).start()
+
+    def to_far(k, q, xo):
+        def send():
+            if team > 1:
+                mate_copy(k, q, xo).wait_recv()
+                got = got_mate[k - 1, lane_of(q, xo)]
+                part[xo, q, block(k)] = part[xo, q, block(k)] + got
+            far_copy(k, q, xo).start()
+
+        if team > 1:
+            pl.when(jnp.logical_not(hands_over(k)))(send)
+        else:
+            send()
+
+    def arrived(q, xo):
+        got = []
+        for k in range(1, team):
+            mate_copy(k, q, xo).wait_recv()
+            got.append(got_mate[k - 1, lane_of(q, xo)])
+        for k in range(team, zs, team):
+            far_copy(k, q, xo).wait_recv()
+            got.append(got_far[teams - k // team - 1, lane_of(q, xo)])
+        return functools.reduce(jnp.add, got)
+
+    def along_z(piece):
+        contribute(0, piece)
+        for q in piece:
+            for k in order:
+                part[0, q, block(k)] = gather(k, q)
+                to_mate(k, q, 0)
+            for k in range(team, zs):
+                to_far(k, q, 0)
+
+    def load(piece):
+        at = columns(piece)
+        u_loads[loads.index(piece)].wait()
+        u_high[:, at], u_low[:, at] = split(u_buf[:, at])
+
     for p, piece in enumerate(pieces):
-        at = columns(piece)
-        u_loads[p].wait()
-        u_high[:, at], u_low[:, at] = split(u_buf[:, at])
+        load(piece)
         for xo in range(1, xs):
             contribute(xo, piece)
         if p == 0:
@@ -271,42 +331,33 @@
             for k in order:
                 for xo in range(1, xs):
                     x_copy(xo, q, k).start()
-    for q in range(chunks):
-        for xo in range(1, xs):
-            x_copy(xo, q, 0).start()
-    for hop in range(zs - 1):
-        pass_on(hop)
-    place(0)
-
-    def gather(k, q):
-        total = part[0, q, block(k)]
-        for xo in range(1, xs):
-            x_copy(xo, q, k).wait_recv()
-            total = total + got_x[xo - 1, q, block(k)]
-        return total
-
-    for piece in pieces:
-        contribute(0, piece)
-        for q in piece:
-            for k in order:
-                part[0, q, block(k)] = gather(k, q)
-                if k < team:
-                    mate_copy(k, q).start()
-                elif team > 1:
-                    @pl.when(hands_over(k))
-                    def _(k=k, q=q):
-                        mate_copy(k, q).start()
-            for k in range(team, zs):
-                def send_far(k=k, q=q):
-                    if team > 1:
-                        mate_copy(k, q).wait_recv()
-                        part[0, q, block(k)] = part[0, q, block(k)] + got_mate[k - 1, q]
-                    far_copy(k, q).start()
-
-                if team > 1:
-                    pl.when(jnp.logical_not(hands_over(k)))(send_far)
-                else:
-                    send_far()
+        if p == 0:
+            place(0)
+            if early:
+                load(range(early))
+                for xo in range(xs):
+                    contribute(xo, range(early))
+                for q in range(early):
+                    for k in order:
+                        for xo in range(xs):
+                            to_mate(k, q, xo)
+        if p == 1:
+            for hop in range(zs - 1):
+                pass_on(hop)
+            for q in range(early):
+                for k in range(team, zs):
+                    for xo in range(xs):
+                        to_far(k, q, xo)
+        if p == len(pieces) - 1:
+            for q in range(early):
+                for xo in range(1, xs):
+                    part[xo, q, block(0)] = part[xo, q, block(0)] + arrived(q, xo)
+            for q in range(chunks):
+                for xo in range(1, xs):
+                    x_copy(xo, q, 0).start()
+        if p > 0:
+            along_z(pieces[p - 1])
+    along_z(pieces[-1])
     near_loads[1].wait()
     leaf_gram = jnp.zeros((own_rows, own_rows), F32)
     for q in range(chunks):
@@ -314,14 +365,7 @@
         near = [
             diag[c : c + 1, at] * sketch[c * rank : (c + 1) * rank, at] for c in range(local)
         ]
-        total = gather(0, q) + jnp.concatenate(near, axis=0)
-        for k in range(1, team):
-            mate_copy(k, q).wait_recv()
-            total = total + got_mate[k - 1, q]
-        for k in range(team, zs, team):
-            slot = teams - k // team - 1
-            far_copy(k, q).wait_recv()
-            total = total + got_far[slot, q]
+        total = gather(0, q) + jnp.concatenate(near, axis=0) + arrived(q, 0)
         sample[:, at] = total
         leaf_gram = leaf_gram + dot(total, total, NT, HIGHEST)
 
@@ -383,19 +427,20 @@
 
     for q in range(chunks):
         for xo in range(1, xs):
-            for k in range(zs):
+            for k in range(1 if q < early else zs):
                 x_copy(xo, q, k).wait_send()
-        for k in range(1, team):
-            mate_copy(k, q).wait_send()
-        for k in range(team, zs):
-            def sent(copy, k=k, q=q):
-                copy(k, q).wait_send()
-
-            if team > 1:
-                pl.when(hands_over(k))(functools.partial(sent, mate_copy))
-                pl.when(jnp.logical_not(hands_over(k)))(functools.partial(sent, far_copy))
-            else:
-                sent(far_copy)
+        for xo in range(xs if q < early else 1):
+            for k in range(1, team):
+                mate_copy(k, q, xo).wait_send()
+            for k in range(team, zs):
+                def sent(copy, k=k, q=q, xo=xo):
+                    copy(k, q, xo).wait_send()
+
+                if team > 1:
+                    pl.when(hands_over(k))(functools.partial(sent, mate_copy))
+                    pl.when(jnp.logical_not(hands_over(k)))(functools.partial(sent, far_copy))
+                else:
+                    sent(far_copy)
     for o in range(1, members):
         g_copy(o).wait_send()
     for o in range(1, groups):
@@ -425,6 +470,8 @@
     zs = members // xs
     team = 2 if zs % 2 == 0 else 1
     chunks = leaf_rows // WIDTH
+    early = early_of(chunks, xs, zs)
+    lanes = chunks + (xs - 1) * early
     slots = blocks * rank
     own = local * rank
     vmem = pl.BlockSpec(memory_space=pltpu.VMEM)
@@ -451,21 +498,21 @@
             pltpu.VMEM((xs, zs * own, slots), BF16),
             pltpu.VMEM((xs, chunks, zs * own, WIDTH), F32),
             pltpu.VMEM((max(xs - 1, 1), chunks, zs * own, WIDTH), F32),
-            pltpu.VMEM((max(zs - 1, 1), chunks, own, WIDTH), F32),
-            pltpu.VMEM((max(zs // team - 1, 1), chunks, own, WIDTH), F32),
+            pltpu.VMEM((max(zs - 1, 1), lanes, own, WIDTH), F32),
+            pltpu.VMEM((max(zs // team - 1, 1), lanes, own, WIDTH), F32),
             pltpu.VMEM((own, leaf_rows), F32),
             pltpu.VMEM((8, rank * rank // 8), F32),
             pltpu.VMEM((members, 8, rank * rank // 8), F32),
             pltpu.VMEM((8, rank * rank // 8), F32),
             pltpu.VMEM((groups, 8, rank * rank // 8), F32),
             pltpu.VMEM((local, rank, rank), F32),
-            dma((4 + V_PARTS + len(pieces_of(chunks)),)),
+            dma((5 + V_PARTS + len(pieces_of(chunks, early)),)),
             dma((max(xs - 1, 1), chunks, zs)),
             dma((max(xs - 1, 1), chunks, zs)),
-            dma((max(zs - 1, 1), chunks)),
-            dma((max(zs - 1, 1), chunks)),
-            dma((max(zs - team, 1), chunks)),
-            dma((max(zs // team - 1, 1), chunks)),
+            dma((max(zs - 1, 1), lanes)),
+            dma((max(zs - 1, 1), lanes)),
+            dma((max(zs - team, 1), lanes)),
+            dma((max(zs // team - 1, 1), lanes)),
             dma((members - 1,)),
             dma((members - 1,)),
             dma((groups - 1,)),

time: 47.7 us -> 45.7 us (0.958)
  Pallas kernels: 46.9 us -> 44.9 us
    pallas_call x1, Pallas kernels: 43.9 us -> 41.9 us  [body(): pl.pallas_call(functools.partial(kernel, xs, local), out_shape=(jax.Shape...]
where the time goes in v3:
time: 45.7 us; the launch traced here: 45.6 us
  Pallas kernels  44.9 us (98%)
  between operations  0.64 us (1%)
    pallas_call x1, Pallas kernels, body(): pl.pallas_call(functools.partial(kernel, xs, local), out_shape=(jax.Shape...  41.9 us
    pallas_call x1, Pallas kernels, body(): pl.pallas_call(finish, out_shape=(jax.ShapeDtypeStruct((local, rank, leaf...  3.01 us

profile of v3, /device:TPU:0, one launch (start us, length us, event | category | flops | bytes accessed | tf_op | source)
XLA Modules:
  0.0 45.6 jit_solution(13524160963567264691)
XLA Ops:
  0.6 41.9 %shard_map.85 = (f32[64,1024]{1,0:T(8,128)}, f32[6,32,32]{2,1,0:T(8,128)}) custom-call(f32[768,1024]{1,0:T(8,128)} %bitcast.3, f32[768,1024]{1,0:T(8,128)} %bitcast.4, f32[64,1024]{1,0:T(8,128)} %bitcast.5, f32[2,1024]{1,0:T(2,128)} %diag_hbm.1, s32[24]{0:T(128)} %row_hbm.1, s32[2]{0:T(128)} %count_hbm.1), custom_call_target="tpu_custom_call" | custom-call | tf_op jit(solution)/shard_map/pallas_call | solution.py:480
  42.6 3.0 %shard_map.86 = (f32[2,32,1024]{2,1,0:T(8,128)}, f32[2,32,32]{2,1,0:T(8,128)}, f32[1,32,32]{2,1,0:T(8,128)}) custom-call(f32[64,1024]{1,0:T(8,128)} %get-tuple-element.5.sample_hbm, f32[6,32,32]{2,1,0:T(8,128)} %get-tuple-element.6.squares), custom_call_target="tpu_custom_call" | custom-call | tf_op jit(solution)/shard_map/pallas_call | solution.py:533

commit v4 on v3

--- a/solution.py
+++ b/solution.py
@@ -16,8 +16,8 @@
 NT = (((1,), (1,)), ((), ()))
 WIDTH = 128
 PAIR = 2
-V_PARTS = 3
-PIVOTS = 8
+V_PARTS = 1
+PIVOTS = 16
 
 
 def dot(a, b, dims, precision=None):
@@ -32,6 +32,13 @@
 def dot3(a, b, dims):
     (ah, al), (bh, bl) = a, b
     return dot(ah, bh, dims) + dot(ah, bl, dims) + dot(al, bh, dims)
+
+
+def dot3_stacked(a, b, dims):
+    (high, rest), (bh, bl) = a, b
+    rows = high.shape[0]
+    both = dot(jnp.concatenate([high, rest], axis=0), bh, dims)
+    return both[:rows] + both[rows:] + dot(high, bl, dims)
 
 
 def pack(square):
@@ -139,7 +146,7 @@
         pltpu.make_async_copy(row_hbm, block_row, load_sems.at[2 + V_PARTS]),
         pltpu.make_async_copy(count_hbm, col_count, load_sems.at[3 + V_PARTS]),
     ]
-    for load in index_loads + near_loads[:1] + v_loads + u_loads + near_loads[1:]:
+    for load in index_loads + near_loads[:1] + v_loads + u_loads[:1] + u_loads[1:] + near_loads[1:]:
         load.start()
     barrier = pltpu.get_barrier_semaphore()
     for xo in range(1, xs):
@@ -197,7 +204,7 @@
     parts = []
     for i in range(V_PARTS):
         v_loads[i].wait()
-        parts.append(dot3(sketch_parts, split(v_buf[i * v_rows : (i + 1) * v_rows]), NT))
+        parts.append(dot3_stacked(sketch_parts, split(v_buf[i * v_rows : (i + 1) * v_rows]), NT))
     every = jnp.concatenate(parts, axis=1)
     coupling = jnp.zeros((rank, slots), F32)
     for c in range(local):
@@ -222,13 +229,30 @@
         for h, q in enumerate(piece):
             part[xo, q] = out[:, h * WIDTH : (h + 1) * WIDTH]
 
-    def x_copy(xo, q, k):
-        at = pl.ds(k * own_rows, own_rows)
+    def runs(q):
+        if q in pieces[-1]:
+            return [(k, n) for k, n in ((team, zs - team), (1, team - 1)) if n]
+        return [(1, zs - 1)]
+
+    def x_copy(xo, q, run):
+        k, n = run
+        at = pl.ds(k * own_rows, n * own_rows)
         return pltpu.make_async_remote_copy(
             src_ref=part.at[xo, q, at],
             dst_ref=got_x.at[xo - 1, q, at],
             send_sem=x_send.at[xo - 1, q, k],
             recv_sem=x_recv.at[xo - 1, q, k],
+            device_id={"dev": z * xs + (x + xo) % xs},
+            device_id_type=MESH,
+        )
+
+    def own_copy(xo, piece):
+        at = (pl.ds(piece.start, len(piece)), pl.ds(0, own_rows))
+        return pltpu.make_async_remote_copy(
+            src_ref=part.at[xo, *at],
+            dst_ref=got_x.at[xo - 1, *at],
+            send_sem=x_send.at[xo - 1, piece.start, 0],
+            recv_sem=x_recv.at[xo - 1, piece.start, 0],
             device_id={"dev": z * xs + (x + xo) % xs},
             device_id_type=MESH,
         )
@@ -271,7 +295,14 @@
     def gather(k, q):
         total = part[0, q, block(k)]
         for xo in range(1, xs):
-            x_copy(xo, q, k).wait_recv()
+            if k == 0:
+                for piece in loads:
+                    if piece.start == q:
+                        own_copy(xo, piece).wait_recv()
+            else:
+                for run in runs(q):
+                    if k == next(o for o in order if run[0] <= o < run[0] + run[1]):
+                        x_copy(xo, q, run).wait_recv()
             total = total + got_x[xo - 1, q, block(k)]
         return total
 
@@ -328,9 +359,9 @@
             pl.semaphore_wait(barrier, xs - 1 + groups - 1 + near_z)
             greet(relay.at[0])
         for q in piece:
-            for k in order:
+            for run in runs(q):
                 for xo in range(1, xs):
-                    x_copy(xo, q, k).start()
+                    x_copy(xo, q, run).start()
         if p == 0:
             place(0)
             if early:
@@ -352,9 +383,9 @@
             for q in range(early):
                 for xo in range(1, xs):
                     part[xo, q, block(0)] = part[xo, q, block(0)] + arrived(q, xo)
-            for q in range(chunks):
+            for own in sorted(loads, key=lambda r: r.start):
                 for xo in range(1, xs):
-                    x_copy(xo, q, 0).start()
+                    own_copy(xo, own).start()
         if p > 0:
             along_z(pieces[p - 1])
     along_z(pieces[-1])
@@ -427,8 +458,11 @@
 
     for q in range(chunks):
         for xo in range(1, xs):
-            for k in range(1 if q < early else zs):
-                x_copy(xo, q, k).wait_send()
+            for run in runs(q) if q >= early else []:
+                x_copy(xo, q, run).wait_send()
+            for piece in loads:
+                if piece.start == q:
+                    own_copy(xo, piece).wait_send()
         for xo in range(xs if q < early else 1):
             for k in range(1, team):
                 mate_copy(k, q, xo).wait_send()

time: 45.7 us -> 44.8 us (0.980)
  Pallas kernels: 44.9 us -> 44 us
    pallas_call x1, Pallas kernels: 41.9 us -> 41.1 us  [body(): pl.pallas_call(functools.partial(kernel, xs, local), out_shape=(jax.Shape...]
where the time goes in v4:
time: 44.8 us; the launch traced here: 44.6 us
  Pallas kernels  44 us (98%)
  between operations  0.64 us (1%)
    pallas_call x1, Pallas kernels, body(): pl.pallas_call(functools.partial(kernel, xs, local), out_shape=(jax.Shape...  41.1 us
    pallas_call x1, Pallas kernels, body(): pl.pallas_call(finish, out_shape=(jax.ShapeDtypeStruct((local, rank, leaf...  2.91 us

profile of v4, /device:TPU:0, one launch (start us, length us, event | category | flops | bytes accessed | tf_op | source)
XLA Modules:
  0.0 44.6 jit_solution(390416664789419317)
XLA Ops:
  0.6 41.1 %shard_map.85 = (f32[64,1024]{1,0:T(8,128)}, f32[6,32,32]{2,1,0:T(8,128)}) custom-call(f32[768,1024]{1,0:T(8,128)} %bitcast.3, f32[768,1024]{1,0:T(8,128)} %bitcast.4, f32[64,1024]{1,0:T(8,128)} %bitcast.5, f32[2,1024]{1,0:T(2,128)} %diag_hbm.1, s32[24]{0:T(128)} %row_hbm.1, s32[2]{0:T(128)} %count_hbm.1), custom_call_target="tpu_custom_call" | custom-call | tf_op jit(solution)/shard_map/pallas_call | solution.py:514
  41.7 2.9 %shard_map.86 = (f32[2,32,1024]{2,1,0:T(8,128)}, f32[2,32,32]{2,1,0:T(8,128)}, f32[1,32,32]{2,1,0:T(8,128)}) custom-call(f32[64,1024]{1,0:T(8,128)} %get-tuple-element.5.sample_hbm, f32[6,32,32]{2,1,0:T(8,128)} %get-tuple-element.6.squares), custom_call_target="tpu_custom_call" | custom-call | tf_op jit(solution)/shard_map/pallas_call | solution.py:567

commit v5 on v4

--- a/solution.py
+++ b/solution.py
@@ -18,6 +18,7 @@
 PAIR = 2
 V_PARTS = 1
 PIVOTS = 16
+LAG = 1
 
 
 def dot(a, b, dims, precision=None):
@@ -337,14 +338,30 @@
             got.append(got_far[teams - k // team - 1, lane_of(q, xo)])
         return functools.reduce(jnp.add, got)
 
-    def along_z(piece):
-        contribute(0, piece)
-        for q in piece:
+    late = hands_over(team)
+
+    def to_mate_rows(piece):
+        @pl.when(late)
+        def _():
+            for q in piece:
+                for k in range(1, team):
+                    mate_copy(k, q).start()
+
+    def along_z(p):
+        contribute(0, pieces[p])
+        for q in pieces[p]:
             for k in order:
                 part[0, q, block(k)] = gather(k, q)
-                to_mate(k, q, 0)
+                if k >= team:
+                    to_mate(k, q, 0)
+                else:
+                    @pl.when(jnp.logical_not(late))
+                    def _(k=k, q=q):
+                        mate_copy(k, q).start()
             for k in range(team, zs):
                 to_far(k, q, 0)
+        if p >= LAG:
+            to_mate_rows(pieces[p - LAG])
 
     def load(piece):
         at = columns(piece)
@@ -387,8 +404,10 @@
                 for xo in range(1, xs):
                     own_copy(xo, own).start()
         if p > 0:
-            along_z(pieces[p - 1])
-    along_z(pieces[-1])
+            along_z(p - 1)
+    along_z(len(pieces) - 1)
+    for piece in pieces[max(len(pieces) - LAG, 0) :]:
+        to_mate_rows(piece)
     near_loads[1].wait()
     leaf_gram = jnp.zeros((own_rows, own_rows), F32)
     for q in range(chunks):

time: 44.8 us -> 44.5 us (level)
  no operation moved by 1% of the time
where the time goes in v5:
time: 44.5 us; the launch traced here: 44.3 us
  Pallas kernels  43.7 us (98%)
  between operations  0.64 us (1%)
    pallas_call x1, Pallas kernels, body(): pl.pallas_call(functools.partial(kernel, xs, local), out_shape=(jax.Shape...  40.7 us
    pallas_call x1, Pallas kernels, body(): pl.pallas_call(finish, out_shape=(jax.ShapeDtypeStruct((local, rank, leaf...  2.91 us

profile of v5, /device:TPU:0, one launch (start us, length us, event | category | flops | bytes accessed | tf_op | source)
XLA Modules:
  0.0 44.3 jit_solution(50662059108471087)
XLA Ops:
  0.6 40.7 %shard_map.85 = (f32[64,1024]{1,0:T(8,128)}, f32[6,32,32]{2,1,0:T(8,128)}) custom-call(f32[768,1024]{1,0:T(8,128)} %bitcast.3, f32[768,1024]{1,0:T(8,128)} %bitcast.4, f32[64,1024]{1,0:T(8,128)} %bitcast.5, f32[2,1024]{1,0:T(2,128)} %diag_hbm.1, s32[24]{0:T(128)} %row_hbm.1, s32[2]{0:T(128)} %count_hbm.1), custom_call_target="tpu_custom_call" | custom-call | tf_op jit(solution)/shard_map/pallas_call | solution.py:533
  41.4 2.9 %shard_map.86 = (f32[2,32,1024]{2,1,0:T(8,128)}, f32[2,32,32]{2,1,0:T(8,128)}, f32[1,32,32]{2,1,0:T(8,128)}) custom-call(f32[64,1024]{1,0:T(8,128)} %get-tuple-element.5.sample_hbm, f32[6,32,32]{2,1,0:T(8,128)} %get-tuple-element.6.squares), custom_call_target="tpu_custom_call" | custom-call | tf_op jit(solution)/shard_map/pallas_call | solution.py:586
